TPU v7x, 32 devices: a whole 2x2x4 slice. The times are simulated.
32 devices in a mesh: seq: 8 (over z, x), panel: 4 (over y, core).
Axes of the slice: x: 2, y: 2, z: 4, core: 2. Of those that a mesh axis runs over, the one named last changes fastest.
Arguments:
- tokens: bfloat16 [512, 8192], P(('seq', 'panel')), may hold values from -6 to 6
- gate_weight: bfloat16 [2048, 8192], P(('seq', 'panel')), may hold values from -0.0625 to 0.0625
- up_weight: bfloat16 [2048, 8192], P(('seq', 'panel')), may hold values from -0.0625 to 0.0625
- gate_mask: int32 [32, 128], P(('seq', 'panel')), may hold values from 0 to 1, as said below
- up_mask: int32 [32, 128], P(('seq', 'panel')), may hold values from 0 to 1, as said below
Outputs:
- hidden: bfloat16 [512, 2048], P(('seq', 'panel'))
Inputs may be any that keep to these rules, and one draw needn't show every extreme that they name: Every block row of gate_mask keeps between 32 and 96 of its 128 blocks; some block row keeps exactly 96. Every block row of up_mask keeps between 32 and 96 of its 128 blocks; some block row keeps exactly 96.
All inputs are finite; a program needn't handle non-finite values.
Results may differ from a plain program's by a relative error of at most 0.0012.
Values may be sent and summed in bfloat16 or wider, within the bound.
A program may use at most 128 MiB of HBM per device.

v0:
```python
import jax
import jax.numpy as jnp
from jax import lax
from jax.sharding import PartitionSpec as P


def passed_along(block, axis, distance):
    devices = range(lax.axis_size(axis))
    route = [((i - distance) % len(devices), i) for i in devices]
    return lax.ppermute(block, axis, route)


def masked_weight(weight, mask):
    row_blocks, col_blocks = mask.shape
    shaped = weight.reshape(
        row_blocks, weight.shape[0] // row_blocks, col_blocks, weight.shape[1] // col_blocks
    )
    return (shaped * mask.astype(jnp.bfloat16)[:, None, :, None]).reshape(weight.shape)


def project(token_rows, weight):
    return lax.dot_general(
        token_rows, weight, (((1,), (1,)), ((), ())), preferred_element_type=jnp.float32
    )


def gated_block(token_rows, gate_part, up_part):
    gate = project(token_rows, gate_part)
    up_values = project(token_rows, up_part)
    return (jax.nn.silu(gate) * up_values).astype(jnp.bfloat16)


def collect_panels(stacked):
    panel_count = lax.axis_size("panel")
    collected = [(stacked, 0)]
    moving = stacked
    for distance in range(1, panel_count):
        moving = passed_along(moving, "panel", 1)
        collected.append((moving, distance))
    return collected


def shards(tokens, gate_weight, up_weight, gate_mask, up_mask):
    panel_count = lax.axis_size("panel")
    my_panel = lax.axis_index("panel")
    width_rows = gate_weight.shape[0]
    stacked = jnp.stack([masked_weight(gate_weight, gate_mask), masked_weight(up_weight, up_mask)])
    collected = collect_panels(stacked)
    gathered = lax.all_gather(tokens, "seq", axis=0, tiled=True)
    tile = jnp.zeros((gathered.shape[0], panel_count * width_rows), jnp.bfloat16)
    for pair, distance in collected:
        source = (my_panel - distance) % panel_count
        result = gated_block(gathered, pair[0], pair[1])
        tile = lax.dynamic_update_slice_in_dim(tile, result, source * width_rows, 1)
    return lax.all_to_all(tile, "seq", split_axis=0, concat_axis=1, tiled=True)


def solution(mesh):
    in_specs = (
        P(("seq", "panel"), None),
        P(("seq", "panel"), None),
        P(("seq", "panel"), None),
        P(("seq", "panel"), None),
        P(("seq", "panel"), None),
    )
    out_specs = P(("seq", "panel"), None)
    return jax.shard_map(shards, mesh=mesh, in_specs=in_specs, out_specs=out_specs, check_vma=False)
```

profile of v0, /device:TPU:0, one launch (start us, length us, event | category | flops | bytes accessed | tf_op | source)
XLA Modules:
  0.0 114.7 jit_solution(3382346996524483620)
XLA Ops:
  6.5 0.0 all-gather.2.cloned.1.call-start
  6.5 0.7 convert_bitcast_fusion
  7.2 0.1 mul.86
  7.3 0.1 mul.87
  7.4 0.7 convert_bitcast_fusion.1
  8.0 0.1 mul.80
  8.1 0.1 mul.81
  8.2 1.8 %multiply_bitcast_fusion = (bf16[1,64,8192]{2,1,0:T(8,128)(2,1)S(1)}, bf16[1,64,8192]{2,1,0:T(8,128)(2,1)S(1)}) fusion(bf16[64,8192]{1,0:T(8,128)(2,1)} %param.7, bf16[8192]{0:T(1024)(128)(2,1)S(1)} %mul.87, bf16[64,8192]{1,0:T(8,128)(2,1)} %param.6, bf16[8192]{0:T(1024)(128)(2,1)S(1)} %mul.81), kind=kLoop, calls=%fused_computation.17 | loop fusion | flops 1048576 | bytes 4227072 | tf_op jit(solution)/shard_map/mul | solution.py:18
  10.0 0.0 copy-start.1
  10.0 1.5 %pad_maximum_fusion = bf16[2,64,8192]{2,1,0:T(8,128)(2,1)} fusion(bf16[1,64,8192]{2,1,0:T(8,128)(2,1)S(1)} %get-tuple-element.5, bf16[1,64,8192]{2,1,0:T(8,128)(2,1)S(1)} %get-tuple-element.6), kind=kLoop, calls=%fused_computation | loop fusion | flops 1048576 | bytes 4194304 | tf_op jit(solution)/shard_map/stack | solution.py:47
  11.5 0.5 collective-permute-start
  12.0 0.0 all-gather.2.cloned.1.call-update
  12.1 25.8 %collective-permute-done = bf16[2,64,8192]{2,1,0:T(8,128)(2,1)S(1)} collective-permute-done((bf16[2,64,8192]{2,1,0:T(8,128)(2,1)}, bf16[2,64,8192]{2,1,0:T(8,128)(2,1)S(1)}, u32[]{:S(2)}, u32[]{:S(2)}) %collective-permute-start) | collective-permute-done | bytes 2097184 | tf_op jit(solution)/shard_map/ppermute | solution.py:10
  37.9 0.0 copy-start.2
  37.9 0.0 collective-permute-start.1
  38.0 25.5 %collective-permute-done.1 = bf16[2,64,8192]{2,1,0:T(8,128)(2,1)} collective-permute-done((bf16[2,64,8192]{2,1,0:T(8,128)(2,1)S(1)}, bf16[2,64,8192]{2,1,0:T(8,128)(2,1)}, u32[]{:S(2)}, u32[]{:S(2)}) %collective-permute-start.1) | collective-permute-done | bytes 2097184 | tf_op jit(solution)/shard_map/ppermute | solution.py:10
  63.5 0.0 collective-permute-start.2
  63.5 0.0 copy-done.2
  63.5 0.4 all-gather.2.cloned.1.call-done
  63.9 0.0 copy-done.1
  63.9 0.0 copy-start
  63.9 2.6 %convolution_bitcast_fusion.7 = f32[128,64]{0,1:T(8,128)S(1)} fusion(bf16[128,8192]{1,0:T(8,128)(2,1)} %all-gather.2.cloned.1.call-done, bf16[64,8192]{1,0:T(8,128)(2,1)S(1)} %copy-done.1, bf16[8192]{0:T(1024)(128)(2,1)S(1)} %mul.81), kind=kOutput, calls=%fused_computation.9 | convolution fusion | flops 134742016 | bytes 3194880 | tf_op jit(solution)/shard_map/dot_general | solution.py:22
  66.4 0.0 copy-done
  66.5 2.1 %fusion.1 = bf16[128,64]{0,1:T(8,128)(2,1)S(1)} fusion(bf16[128,8192]{1,0:T(8,128)(2,1)S(1)} %copy-done, bf16[64,8192]{1,0:T(8,128)(2,1)} %param.7, bf16[8192]{0:T(1024)(128)(2,1)S(1)} %mul.87, f32[128,64]{0,1:T(8,128)S(1)} %convolution_bitcast_fusion.7), kind=kOutput, calls=%fused_computation.10 | convolution fusion | flops 134791168 | bytes 3211264 | tf_op jit(solution)/shard_map/dot_general | solution.py:22
  68.5 0.1 copy.10
  68.6 0.0 copy-start.3
  68.7 2.2 %convolution_bitcast_fusion.5 = f32[128,64]{0,1:T(8,128)S(1)} fusion(bf16[128,8192]{1,0:T(8,128)(2,1)S(1)} %copy-done, bf16[2,64,8192]{2,1,0:T(8,128)(2,1)} %copy-done.2), kind=kOutput, calls=%fused_computation.6 | convolution fusion | flops 134217728 | bytes 3178496 | tf_op jit(solution)/shard_map/dot_general | solution.py:22
  70.9 0.0 copy-done.3
  70.9 0.8 multiply_convert_fusion.2
  71.7 0.1 copy.11
  71.9 0.2 dynamic_update_slice.12
  72.1 0.4 dynamic_update_slice.13
  72.5 2.1 %convolution_bitcast_fusion.3 = f32[128,64]{0,1:T(8,128)S(1)} fusion(bf16[128,8192]{1,0:T(8,128)(2,1)S(1)} %copy-done, bf16[2,64,8192]{2,1,0:T(8,128)(2,1)} %collective-permute-done.1), kind=kOutput, calls=%fused_computation.4 | convolution fusion | flops 134217728 | bytes 3178496 | tf_op jit(solution)/shard_map/dot_general | solution.py:22
  74.6 2.1 %multiply_convert_fusion.1 = bf16[128,64]{0,1:T(8,128)(2,1)S(1)} fusion(f32[128,64]{0,1:T(8,128)S(1)} %convolution_bitcast_fusion.3, bf16[128,8192]{1,0:T(8,128)(2,1)S(1)} %copy-done, bf16[2,64,8192]{2,1,0:T(8,128)(2,1)} %collective-permute-done.1), kind=kOutput, calls=%fused_computation.24 | convolution fusion | flops 134266880 | bytes 3194880 | tf_op jit(solution)/shard_map/dot_general | solution.py:22
  76.7 0.1 copy.12
  76.8 0.2 dynamic_update_slice.14
  77.0 12.3 %collective-permute-done.2 = bf16[2,64,8192]{2,1,0:T(8,128)(2,1)} collective-permute-done((bf16[2,64,8192]{2,1,0:T(8,128)(2,1)}, bf16[2,64,8192]{2,1,0:T(8,128)(2,1)}, u32[]{:S(2)}, u32[]{:S(2)}) %collective-permute-start.2) | collective-permute-done | bytes 2097184 | tf_op jit(solution)/shard_map/ppermute | solution.py:10
  89.3 2.1 %convolution_bitcast_fusion.1 = f32[128,64]{0,1:T(8,128)S(1)} fusion(bf16[128,8192]{1,0:T(8,128)(2,1)S(1)} %copy-done, bf16[2,64,8192]{2,1,0:T(8,128)(2,1)} %collective-permute-done.2), kind=kOutput, calls=%fused_computation.2 | convolution fusion | flops 134217728 | bytes 3178496 | tf_op jit(solution)/shard_map/dot_general | solution.py:22
  91.3 2.1 %multiply_convert_fusion = bf16[128,64]{0,1:T(8,128)(2,1)S(1)} fusion(f32[128,64]{0,1:T(8,128)S(1)} %convolution_bitcast_fusion.1, bf16[128,8192]{1,0:T(8,128)(2,1)S(1)} %copy-done, bf16[2,64,8192]{2,1,0:T(8,128)(2,1)} %collective-permute-done.2), kind=kOutput, calls=%fused_computation.23 | convolution fusion | flops 134266880 | bytes 3194880 | tf_op jit(solution)/shard_map/dot_general | solution.py:22
  93.4 0.1 copy.13
  93.5 0.4 dynamic_update_slice.15
  94.0 13.3 %all_to_all.19 = bf16[8,16,256]{2,1,0:T(8,128)(2,1)S(1)} all-to-all(bf16[8,16,256]{2,1,0:T(8,128)(2,1)S(1)} %bitcast.64), channel_id=1, replica_groups=mesh['seq'=8,'panel'=4] {'seq'}, dimensions={0} | all-to-all | bytes 131072 | tf_op jit(solution)/shard_map/all_to_all | solution.py:55
  107.3 0.6 copy.15
  (1 shorter events, 0.0 us)
Async XLA Ops:
  6.5 57.3 %all-gather.2.cloned.1.call-start = ((), (), s32[]{:S(2)}) async-start(), calls=%async_computation.1 | async-start | bytes 2359296 | tf_op jit(solution)/shard_map/all_gather | solution.py:49
  10.0 53.8 %copy-start.1 = (bf16[64,8192]{1,0:T(8,128)(2,1)S(1)}, bf16[64,8192]{1,0:T(8,128)(2,1)}, u32[]{:S(2)}) copy-start(bf16[64,8192]{1,0:T(8,128)(2,1)} %param.6) | copy-start | bytes 3145732
  11.5 26.4 %collective-permute-start = (bf16[2,64,8192]{2,1,0:T(8,128)(2,1)}, bf16[2,64,8192]{2,1,0:T(8,128)(2,1)S(1)}, u32[]{:S(2)}, u32[]{:S(2)}) collective-permute-start(bf16[2,64,8192]{2,1,0:T(8,128)(2,1)} %pad_maximum_fusion), channel_id=1, source_target_pairs={{3,0},{0,1},{1,2},{2,3},{7,4},{4,5},{5,6},{6,7},{11,8},{8,9},{9,10... | collective-permute-start | bytes 6291464 | tf_op jit(solution)/shard_map/ppermute | solution.py:10
  37.9 25.6 %copy-start.2 = (bf16[2,64,8192]{2,1,0:T(8,128)(2,1)}, bf16[2,64,8192]{2,1,0:T(8,128)(2,1)S(1)}, u32[]{:S(2)}) copy-start(bf16[2,64,8192]{2,1,0:T(8,128)(2,1)S(1)} %collective-permute-done) | copy-start | bytes 6291460
  37.9 25.6 %collective-permute-start.1 = (bf16[2,64,8192]{2,1,0:T(8,128)(2,1)S(1)}, bf16[2,64,8192]{2,1,0:T(8,128)(2,1)}, u32[]{:S(2)}, u32[]{:S(2)}) collective-permute-start(bf16[2,64,8192]{2,1,0:T(8,128)(2,1)S(1)} %collective-permute-done), channel_id=1, source_target_pairs={{3,0},{0,1},{1,2},{2,3},{7,4},{4,5},{5,6},{6,7},{11,8},{8,9},{9,10... | collective-permute-start | bytes 6291464 | tf_op jit(solution)/shard_map/ppermute | solution.py:10
  63.5 25.8 %collective-permute-start.2 = (bf16[2,64,8192]{2,1,0:T(8,128)(2,1)}, bf16[2,64,8192]{2,1,0:T(8,128)(2,1)}, u32[]{:S(2)}, u32[]{:S(2)}) collective-permute-start(bf16[2,64,8192]{2,1,0:T(8,128)(2,1)} %collective-permute-done.1), channel_id=1, source_target_pairs={{3,0},{0,1},{1,2},{2,3},{7,4},{4,5},{5,6},{6,7},{11,8},{8,9},{9,10... | collective-permute-start | bytes 6291464 | tf_op jit(solution)/shard_map/ppermute | solution.py:10
  63.9 2.6 %copy-start = (bf16[128,8192]{1,0:T(8,128)(2,1)S(1)}, bf16[128,8192]{1,0:T(8,128)(2,1)}, u32[]{:S(2)}) copy-start(bf16[128,8192]{1,0:T(8,128)(2,1)} %all-gather.2.cloned.1.call-done) | copy-start | bytes 6291460
  68.6 2.2 %copy-start.3 = (bf16[2,64,8192]{2,1,0:T(8,128)(2,1)S(1)}, bf16[2,64,8192]{2,1,0:T(8,128)(2,1)}, u32[]{:S(2)}) copy-start(bf16[2,64,8192]{2,1,0:T(8,128)(2,1)} %copy-done.2) | copy-start | bytes 6291460
Sparse Core Ops, SparseCore 0:
  12.2 51.6 all-gather.1
where the time goes:
time: 115 us
  waiting for transfers between devices  64 us (56%)
  matrix products  16 us (14%)
  between operations  13.6 us (12%)
  blocking collectives  13.3 us (12%)
  other arithmetic  4.63 us (4%)
  local copies, waits for them, and re-layouts  2.73 us (2%)
    ppermute x3, waiting for transfers between devices, passed_along(): return lax.ppermute(block, axis, route)  63.6 us
    dot_general x8, matrix products, project(): lax.dot_general(token_rows, weight, (((1,), (1,)), ((), ())), preferred_e...  16 us
    all_to_all x1, blocking collectives, shards(): return lax.all_to_all(tile, 'seq', split_axis=0, concat_axis=1, tiled=True)  13.3 us
    mul x3, other arithmetic, masked_weight(): shaped * mask.astype(jnp.bfloat16)[:, None, :, None]  3.13 us
  transfers between devices with their start and end apart: 4, of which 4 were waited for; matrix products, arithmetic and copies ran while one was open for 11% of the time, Pallas kernels for 0%

commit v1 on v0

--- a/solution.py
+++ b/solution.py
@@ -1,7 +1,17 @@
+import functools
+
 import jax
 import jax.numpy as jnp
 from jax import lax
+from jax.experimental import pallas as pl
+from jax.experimental.pallas import tpu as pltpu
 from jax.sharding import PartitionSpec as P
+
+MESH = pl.DeviceIdType.MESH
+GROUPS = 4
+NZ = 4
+L, XA, XC, XB, YA, YC, YB, DA, DC, DB = range(10)
+NKINDS = 10
 
 
 def passed_along(block, axis, distance):
@@ -40,7 +50,7 @@
     return collected
 
 
-def shards(tokens, gate_weight, up_weight, gate_mask, up_mask):
+def general_shards(tokens, gate_weight, up_weight, gate_mask, up_mask):
     panel_count = lax.axis_size("panel")
     my_panel = lax.axis_index("panel")
     width_rows = gate_weight.shape[0]
@@ -55,13 +65,306 @@
     return lax.all_to_all(tile, "seq", split_axis=0, concat_axis=1, tiled=True)
 
 
+def kernel(
+    tok, gw, uw, gm, um, out,
+    held, w, masks, wide, acc, hid,
+    recv_sem, send_sem, part_send, part_recv, local_sem, out_send, out_recv, out_local,
+):
+    rows, width = tok.shape
+    wrows = gw.shape[0]
+    nblocks = held.shape[0] // rows
+    seq, panel = lax.axis_index("seq"), lax.axis_index("panel")
+    z, x = seq // 2, seq % 2
+    y, core = panel // 2, panel % 2
+    gc = width // GROUPS
+    unit = gc // 8
+
+    def block_of(bz, bx, by):
+        return (bz * 2 + bx) * 2 + by
+
+    def device(bz, bx, by):
+        return (bz * 2 + bx, by * 2 + core)
+
+    me = block_of(z, x, y)
+    xdev, ydev = device(z, 1 - x, y), device(z, x, 1 - y)
+    updev, downdev = device(z + 1, x, y), device(z - 1, x, y)
+    partner = (seq, y * 2 + 1 - core)
+
+    barrier = pltpu.get_barrier_semaphore()
+    for dev in (xdev, ydev, partner):
+        pl.semaphore_signal(barrier, inc=1, device_id=dev, device_id_type=MESH)
+
+    @pl.when(z < NZ - 1)
+    def _():
+        pl.semaphore_signal(barrier, inc=1, device_id=updev, device_id_type=MESH)
+
+    @pl.when(z > 0)
+    def _():
+        pl.semaphore_signal(barrier, inc=1, device_id=downdev, device_id_type=MESH)
+
+    rows_of = lambda b: pl.ds(pl.multiple_of(b * rows, rows), rows)
+    own = pl.ds(pl.multiple_of(core * wrows, wrows), wrows)
+    own_up = pl.ds(pl.multiple_of((2 + core) * wrows, wrows), wrows)
+    locals_ = [
+        pltpu.make_async_copy(gw, w.at[own], local_sem.at[0]),
+        pltpu.make_async_copy(uw, w.at[own_up], local_sem.at[1]),
+        pltpu.make_async_copy(gm, masks.at[core], local_sem.at[2]),
+        pltpu.make_async_copy(um, masks.at[2 + core], local_sem.at[3]),
+        pltpu.make_async_copy(tok, held.at[rows_of(me)], local_sem.at[4]),
+    ]
+    for copy in locals_:
+        copy.start()
+
+    links = (z > 0).astype(jnp.int32) + (z < NZ - 1).astype(jnp.int32)
+    pl.semaphore_wait(barrier, 3 + links)
+
+    def cols(g, first, last):
+        return pl.ds(g * gc + first * unit, (last - first) * unit)
+
+    ALL, A, B, C = (0, 8), (0, 3), (3, 5), (5, 8)
+    AB, BC = (0, 4), (4, 8)
+    sends = []
+
+    def when(cond):
+        return pl.when(cond) if cond is not None else (lambda f: f())
+
+    def send(g, origin, part, dev, kind, oz, cond=None):
+        index = len(sends)
+        span = cols(g, *part)
+        src = tok.at[:, span] if origin is None else held.at[rows_of(origin), span]
+        at = me if origin is None else origin
+        copy = pltpu.make_async_remote_copy(
+            src_ref=src, dst_ref=held.at[rows_of(at), span],
+            send_sem=send_sem.at[index], recv_sem=recv_sem.at[g, kind, oz],
+            device_id=dev, device_id_type=MESH,
+        )
+        sends.append((copy, cond))
+        when(cond)(copy.start)
+
+    def await_piece(g, origin, part, kind, oz):
+        ref = held.at[rows_of(origin), cols(g, *part)]
+        pltpu.make_async_copy(ref, ref, recv_sem.at[g, kind, oz]).wait()
+
+    has_up, has_down = z < NZ - 1, z > 0
+
+    def phase0(g):
+        send(g, None, ALL, updev, L, z, has_up)
+        send(g, None, ALL, downdev, L, z, has_down)
+        send(g, None, ALL, xdev, XA, z)
+        send(g, None, ALL, ydev, YA, z)
+
+    def plane(g):
+        bx, by = block_of(z, 1 - x, y), block_of(z, x, 1 - y)
+        await_piece(g, bx, ALL, XA, z)
+        send(g, bx, AB, ydev, DA, z)
+        send(g, bx, B, updev, XB, z, has_up)
+        send(g, bx, B, downdev, XB, z, has_down)
+        await_piece(g, by, ALL, YA, z)
+        send(g, by, BC, xdev, DC, z)
+        send(g, by, B, updev, YB, z, has_up)
+        send(g, by, B, downdev, YB, z, has_down)
+
+    def plane_diagonal(g):
+        bd = block_of(z, 1 - x, 1 - y)
+        await_piece(g, bd, AB, DA, z)
+        await_piece(g, bd, BC, DC, z)
+        send(g, bd, B, updev, DB, z, has_up)
+        send(g, bd, B, downdev, DB, z, has_down)
+
+    def sides(d):
+        if d < 1 or d > NZ - 1:
+            return
+        for up in (True, False):
+            oz = z - d if up else z + d
+            here = oz >= 0 if up else oz <= NZ - 1
+            onward = jnp.logical_and(here, has_up if up else has_down)
+            yield oz, here, (updev if up else downdev), (onward if d < NZ - 1 else False)
+
+    def line(g, d):
+        for oz, here, dev, onward in sides(d):
+            b = block_of(oz, x, y)
+            when(here)(functools.partial(await_piece, g, b, ALL, L, oz))
+            if onward is not False:
+                send(g, b, ALL, dev, L, oz, onward)
+            send(g, b, A, xdev, XA, oz, here)
+            send(g, b, C, ydev, YC, oz, here)
+            send(g, b, C, xdev, XC, oz, here)
+            send(g, b, A, ydev, YA, oz, here)
+
+    def cross(g, d):
+        for oz, here, dev, onward in sides(d):
+            bx, by = block_of(oz, 1 - x, y), block_of(oz, x, 1 - y)
+            when(here)(functools.partial(await_piece, g, bx, A, XA, oz))
+            send(g, bx, A, ydev, DA, oz, here)
+            when(here)(functools.partial(await_piece, g, by, C, YC, oz))
+            send(g, by, C, xdev, DC, oz, here)
+
+    def ride(g, d, which):
+        for oz, here, dev, onward in sides(d):
+            for kind, flip in which:
+                b = block_of(oz, 1 - x if flip[0] else x, 1 - y if flip[1] else y)
+                when(here)(functools.partial(await_piece, g, b, B, kind, oz))
+                if onward is not False:
+                    send(g, b, B, dev, kind, oz, onward)
+
+    XY = ((XB, (1, 0)), (YB, (0, 1)))
+    DD = ((DB, (1, 1)),)
+
+    def leaves(g):
+        for d in range(1, NZ):
+            for oz, here, _, _ in sides(d):
+                def rest(oz=oz):
+                    await_piece(g, block_of(oz, 1 - x, y), C, XC, oz)
+                    await_piece(g, block_of(oz, x, 1 - y), A, YA, oz)
+                    await_piece(g, block_of(oz, 1 - x, 1 - y), A, DA, oz)
+                    await_piece(g, block_of(oz, 1 - x, 1 - y), C, DC, oz)
+                when(here)(rest)
+
+    def multiply(g):
+        span = cols(g, 0, 8)
+        part = lax.dot_general(
+            held[:, span], w[:, span], (((1,), (1,)), ((), ())), preferred_element_type=jnp.float32
+        )
+        acc[...] = part if g == 0 else acc[...] + part
+
+    def phase(g, p):
+        if p == 0:
+            phase0(g)
+        elif p == 1:
+            plane(g)
+            line(g, 1)
+        elif p == 2:
+            plane_diagonal(g)
+            line(g, 2)
+            ride(g, 1, XY)
+            cross(g, 1)
+        elif p == 3:
+            line(g, 3)
+            ride(g, 1, DD)
+            ride(g, 2, XY)
+            cross(g, 2)
+        elif p == 4:
+            ride(g, 2, DD)
+            ride(g, 3, XY)
+            cross(g, 3)
+        else:
+            ride(g, 3, DD)
+            leaves(g)
+            multiply(g)
+
+    def weights():
+        copies = []
+        for i, (src, dst) in enumerate((
+            (gw, w.at[own]), (uw, w.at[own_up]), (gm, masks.at[core]), (um, masks.at[2 + core]),
+        )):
+            copies.append(pltpu.make_async_remote_copy(
+                src_ref=src, dst_ref=dst, send_sem=part_send.at[i], recv_sem=part_recv.at[i],
+                device_id=partner, device_id_type=MESH,
+            ))
+        for copy in copies:
+            copy.start()
+        return copies
+
+    def prune(copies):
+        for copy in copies:
+            copy.wait()
+        for copy in locals_:
+            copy.wait()
+        step = 512
+        block = width // masks.shape[2]
+        row = lax.broadcasted_iota(jnp.int32, (8, masks.shape[2]), 0)
+        table = jnp.zeros((8, masks.shape[2]), jnp.float32)
+        for r in range(4):
+            table = jnp.where(row == r, masks[r].astype(jnp.float32), table)
+        table = table.astype(jnp.bfloat16)
+
+        @pl.loop(0, width // step)
+        def _(i):
+            start = pl.multiple_of(i * step, step)
+            where_ = lax.broadcasted_iota(jnp.int32, (masks.shape[2], step), 0)
+            col = lax.broadcasted_iota(jnp.int32, (masks.shape[2], step), 1) + start
+            first = where_ * block
+            inside = jnp.logical_and(col >= first, col < first + block)
+            select = jnp.where(inside, 1.0, 0.0).astype(jnp.bfloat16)
+            wide[...] = jnp.dot(table, select, preferred_element_type=jnp.float32)
+            for r in range(4):
+                at = (pl.ds(r * wrows, wrows), pl.ds(start, step))
+                keep = jnp.broadcast_to(wide[r:r + 1, :], (wrows, step))
+                w[at] = (w[at].astype(jnp.float32) * keep).astype(jnp.bfloat16)
+
+    for s in range(GROUPS + 5):
+        for g in range(GROUPS):
+            if 0 <= s - g <= 5:
+                phase(g, s - g)
+        if s == 0:
+            copies = weights()
+        if s == 1:
+            prune(copies)
+
+    half = acc.shape[1] // 2
+    gate = acc[:, :half]
+    hid[...] = (gate / (1.0 + jnp.exp(-gate)) * acc[:, half:]).astype(jnp.bfloat16)
+    mine = pl.ds(pl.multiple_of(me * half, half), half)
+    keep_own = pltpu.make_async_copy(hid.at[rows_of(me)], out.at[:, mine], out_local)
+    results = []
+    for k in range(nblocks - 1, 0, -1):
+        dz, dx, dy = k // 4, (k // 2) % 2, k % 2
+        tz, tx, ty = (z + dz) % NZ, (x + dx) % 2, (y + dy) % 2
+        target = block_of(tz, tx, ty)
+        copy = pltpu.make_async_remote_copy(
+            src_ref=hid.at[rows_of(target)], dst_ref=out.at[:, mine],
+            send_sem=out_send.at[k], recv_sem=out_recv.at[k],
+            device_id=device(tz, tx, ty), device_id_type=MESH,
+        )
+        copy.start()
+        results.append(k)
+    keep_own.start()
+    for copy, cond in sends:
+        when(cond)(copy.wait_send)
+    for k in results:
+        dz, dx, dy = k // 4, (k // 2) % 2, k % 2
+        source = block_of((z + NZ - dz) % NZ, (x + dx) % 2, (y + dy) % 2)
+        ref = out.at[:, pl.ds(pl.multiple_of(source * half, half), half)]
+        pltpu.make_async_copy(ref, ref, out_recv.at[k]).wait()
+        sent = hid.at[rows_of(source)]
+        pltpu.make_async_copy(sent, sent, out_send.at[k]).wait()
+    keep_own.wait()
+
+
+NSENDS = GROUPS * 64
+
+
+def shards(tokens, gate_weight, up_weight, gate_mask, up_mask):
+    rows, width = tokens.shape
+    wrows = gate_weight.shape[0]
+    blocks = lax.axis_size("seq") * lax.axis_size("panel") // 2
+    hidden = lax.axis_size("seq") * lax.axis_size("panel") * wrows
+    dma = pltpu.SemaphoreType.DMA
+    return pl.pallas_call(
+        kernel,
+        out_shape=jax.ShapeDtypeStruct((rows, hidden), jnp.bfloat16),
+        in_specs=[pl.BlockSpec(memory_space=pl.ANY)] * 5,
+        out_specs=pl.BlockSpec(memory_space=pl.ANY),
+        scratch_shapes=[
+            pltpu.VMEM((blocks * rows, width), jnp.bfloat16),
+            pltpu.VMEM((4 * wrows, width), jnp.bfloat16),
+            pltpu.VMEM((4, 1, gate_mask.shape[1]), jnp.int32),
+            pltpu.VMEM((8, 512), jnp.float32),
+            pltpu.VMEM((blocks * rows, 4 * wrows), jnp.float32),
+            pltpu.VMEM((blocks * rows, 2 * wrows), jnp.bfloat16),
+            dma((GROUPS, NKINDS, NZ)),
+            dma((NSENDS,)),
+            dma((4,)), dma((4,)), dma((5,)),
+            dma((blocks,)), dma((blocks,)), dma,
+        ],
+        compiler_params=pltpu.CompilerParams(collective_id=0, has_side_effects=True),
+    )(tokens, gate_weight, up_weight, gate_mask, up_mask)
+
+
 def solution(mesh):
-    in_specs = (
-        P(("seq", "panel"), None),
-        P(("seq", "panel"), None),
-        P(("seq", "panel"), None),
-        P(("seq", "panel"), None),
-        P(("seq", "panel"), None),
+    spec = P(("seq", "panel"), None)
+    fits = mesh.shape["seq"] == 2 * NZ and mesh.shape["panel"] == 4
+    body = shards if fits else general_shards
+    return jax.shard_map(
+        body, mesh=mesh, in_specs=(spec,) * 5, out_specs=spec, check_vma=False
     )
-    out_specs = P(("seq", "panel"), None)
-    return jax.shard_map(shards, mesh=mesh, in_specs=in_specs, out_specs=out_specs, check_vma=False)

time: 115 us -> 54 us (0.47)
  waiting for transfers between devices: 64 us -> 0 us
  Pallas kernels: 0 us -> 52.3 us
  matrix products: 16 us -> 0 us
  between operations: 13.6 us -> 0.01 us
  blocking collectives: 13.3 us -> 0 us
  other arithmetic: 4.63 us -> 0 us
  local copies, waits for them, and re-layouts: 2.73 us -> 1.47 us
    ppermute x3 -> x0, waiting for transfers between devices: 63.6 us -> none  [passed_along(): return lax.ppermute(block, axis, route)]
    pallas_call x0 -> x1, Pallas kernels: none -> 52.3 us  [shards(): pl.pallas_call(kernel, out_shape=jax.ShapeDtypeStruct((rows, hidden), jnp...]
    dot_general x8 -> x0, matrix products: 16 us -> none  [project(): lax.dot_general(token_rows, weight, (((1,), (1,)), ((), ())), preferred_e...]
    all_to_all x1 -> x0, blocking collectives: 13.3 us -> none  [shards(): return lax.all_to_all(tile, 'seq', split_axis=0, concat_axis=1, tiled=True)]
    mul x3 -> x0, other arithmetic: 3.13 us -> none  [masked_weight(): shaped * mask.astype(jnp.bfloat16)[:, None, :, None]]
    another operation x1 -> x0, other arithmetic: 1.51 us -> none  [shards(): jnp.stack([masked_weight(gate_weight, gate_mask), masked_weight(up_weight...]
    unnamed x8 -> x1, local copies, waits for them, and re-layouts: 0.02 us -> 1.47 us
    dynamic_update_slice x4 -> x0, local copies, waits for them, and re-layouts: 1.27 us -> none  [shards(): tile = lax.dynamic_update_slice_in_dim(tile, result, source * width_rows, 1)]
  transfers between devices with their start and end apart: 4 -> 0, of which waited for: 4 -> 0; matrix products, arithmetic and copies ran while one was open for 11% -> 0% of each run, Pallas kernels for 0% -> 0%
where the time goes in v1:
time: 54 us; the launch traced here: 53.8 us
  Pallas kernels  52.3 us (97%)
  local copies, waits for them, and re-layouts  1.47 us (3%)
    pallas_call x1, Pallas kernels, shards(): pl.pallas_call(kernel, out_shape=jax.ShapeDtypeStruct((rows, hidden), jnp...  52.3 us
    unnamed x1, local copies, waits for them, and re-layouts  1.47 us

profile of v1, /device:TPU:0, one launch (start us, length us, event | category | flops | bytes accessed | tf_op | source)
XLA Modules:
  0.0 53.8 jit_solution(6765614174107045491)
XLA Ops:
  0.0 52.3 %shard_map.55 = bf16[16,2048]{1,0:T(8,128)(2,1)} custom-call(bf16[16,8192]{1,0:T(8,128)(2,1)} %tok.1, bf16[64,8192]{1,0:T(8,128)(2,1)} %gw.1, bf16[64,8192]{1,0:T(8,128)(2,1)} %uw.1, s32[1,128]{1,0:T(1,128)} %gm.1, s32[1,128]{1,0:T(1,128)} %um.1), custom_call_target="tpu_custom_call" | custom-call | tf_op jit(solution)/shard_map/pallas_call | solution.py:343
  52.4 1.5 %copy.7 = bf16[16,2048]{1,0:T(8,128)(2,1)} copy(bf16[16,2048]{1,0:T(8,128)(2,1)} %shard_map.55) | data formatting | bytes 131072

commit v2 on v1

v2 whole, which is shorter than its diff:
```python
import functools

import jax
import jax.numpy as jnp
from jax import lax
from jax.experimental import pallas as pl
from jax.experimental.pallas import tpu as pltpu
from jax.sharding import PartitionSpec as P

MESH = pl.DeviceIdType.MESH
RIDING = 14
NZ = 4
L, LC, X, X2, Y, Y2, DA, DC, R, R2 = range(10)
NKINDS = 10


def passed_along(block, axis, distance):
    devices = range(lax.axis_size(axis))
    route = [((i - distance) % len(devices), i) for i in devices]
    return lax.ppermute(block, axis, route)


def masked_weight(weight, mask):
    row_blocks, col_blocks = mask.shape
    shaped = weight.reshape(
        row_blocks, weight.shape[0] // row_blocks, col_blocks, weight.shape[1] // col_blocks
    )
    return (shaped * mask.astype(jnp.bfloat16)[:, None, :, None]).reshape(weight.shape)


def project(token_rows, weight):
    return lax.dot_general(
        token_rows, weight, (((1,), (1,)), ((), ())), preferred_element_type=jnp.float32
    )


def gated_block(token_rows, gate_part, up_part):
    gate = project(token_rows, gate_part)
    up_values = project(token_rows, up_part)
    return (jax.nn.silu(gate) * up_values).astype(jnp.bfloat16)


def collect_panels(stacked):
    panel_count = lax.axis_size("panel")
    collected = [(stacked, 0)]
    moving = stacked
    for distance in range(1, panel_count):
        moving = passed_along(moving, "panel", 1)
        collected.append((moving, distance))
    return collected


def general_shards(tokens, gate_weight, up_weight, gate_mask, up_mask):
    panel_count = lax.axis_size("panel")
    my_panel = lax.axis_index("panel")
    width_rows = gate_weight.shape[0]
    stacked = jnp.stack([masked_weight(gate_weight, gate_mask), masked_weight(up_weight, up_mask)])
    collected = collect_panels(stacked)
    gathered = lax.all_gather(tokens, "seq", axis=0, tiled=True)
    tile = jnp.zeros((gathered.shape[0], panel_count * width_rows), jnp.bfloat16)
    for pair, distance in collected:
        source = (my_panel - distance) % panel_count
        result = gated_block(gathered, pair[0], pair[1])
        tile = lax.dynamic_update_slice_in_dim(tile, result, source * width_rows, 1)
    return lax.all_to_all(tile, "seq", split_axis=0, concat_axis=1, tiled=True)


def kernel(
    tok, gw, uw, gm, um, out,
    held, w, masks, wide, hid,
    recv_sem, send_sem, part_send, part_recv, local_sem, out_send, out_recv, out_local,
):
    rows, width = tok.shape
    wrows = gw.shape[0]
    seq, panel = lax.axis_index("seq"), lax.axis_index("panel")
    z, x = seq // 2, seq % 2
    y, core = panel // 2, panel % 2
    def block_of(bz, bx, by):
        return (bz * 2 + bx) * 2 + by

    def device(bz, bx, by):
        return (bz * 2 + bx, by * 2 + core)

    me = block_of(z, x, y)
    xdev, ydev = device(z, 1 - x, y), device(z, x, 1 - y)
    updev, downdev = device(z + 1, x, y), device(z - 1, x, y)
    partner = (seq, y * 2 + 1 - core)

    barrier = pltpu.get_barrier_semaphore()
    for dev in (xdev, ydev, partner):
        pl.semaphore_signal(barrier, inc=1, device_id=dev, device_id_type=MESH)

    @pl.when(z < NZ - 1)
    def _():
        pl.semaphore_signal(barrier, inc=1, device_id=updev, device_id_type=MESH)

    @pl.when(z > 0)
    def _():
        pl.semaphore_signal(barrier, inc=1, device_id=downdev, device_id_type=MESH)

    rows_of = lambda b: pl.ds(pl.multiple_of(b * rows, rows), rows)
    own = pl.ds(pl.multiple_of(core * wrows, wrows), wrows)
    own_up = pl.ds(pl.multiple_of((2 + core) * wrows, wrows), wrows)
    locals_ = [
        pltpu.make_async_copy(gw, w.at[own], local_sem.at[0]),
        pltpu.make_async_copy(uw, w.at[own_up], local_sem.at[1]),
        pltpu.make_async_copy(gm, masks.at[core], local_sem.at[2]),
        pltpu.make_async_copy(um, masks.at[2 + core], local_sem.at[3]),
        pltpu.make_async_copy(tok, held.at[rows_of(me)], local_sem.at[4]),
    ]
    for copy in locals_:
        copy.start()

    links = (z > 0).astype(jnp.int32) + (z < NZ - 1).astype(jnp.int32)
    pl.semaphore_wait(barrier, 3 + links)

    unit = width // 64
    first = (64 - RIDING) // 2
    ALL, C, A, B = (0, 64), (0, first), (first, 64 - RIDING), (64 - RIDING, 64)
    AB = (first, 64)
    RIDES = (((64 - RIDING, 64 - RIDING // 2), R), ((64 - RIDING // 2, 64), R2))
    sends = []

    def when(cond):
        return pl.when(cond) if cond is not None else (lambda f: f())

    def cols(part):
        return pl.ds(part[0] * unit, (part[1] - part[0]) * unit)

    def plane_rows(oz):
        return pl.ds(pl.multiple_of(oz * 4 * rows, 4 * rows), 4 * rows)

    def copy_piece(src, at, part, dev, kind, oz, cond):
        span = cols(part)
        copy = pltpu.make_async_remote_copy(
            src_ref=src.at[:, span] if src is tok else src.at[at, span], dst_ref=held.at[at, span],
            send_sem=send_sem.at[len(sends)], recv_sem=recv_sem.at[kind, oz],
            device_id=dev, device_id_type=MESH,
        )
        sends.append((copy, cond))
        when(cond)(copy.start)

    def send(origin, part, dev, kind, oz, cond=None):
        copy_piece(held, rows_of(origin), part, dev, kind, oz, cond)

    def await_rows(at, part, kind, oz):
        ref = held.at[at, cols(part)]
        pltpu.make_async_copy(ref, ref, recv_sem.at[kind, oz]).wait()

    def await_piece(origin, part, kind, oz):
        await_rows(rows_of(origin), part, kind, oz)

    has_up, has_down = z < NZ - 1, z > 0
    at_end = jnp.logical_or(z == 0, z == NZ - 1)
    bx, by, bd = block_of(z, 1 - x, y), block_of(z, x, 1 - y), block_of(z, 1 - x, 1 - y)

    def begin():
        mine = rows_of(me)
        for part, kind in ((A, L), (C, LC)):
            copy_piece(tok, mine, part, updev, kind, z, has_up)
            copy_piece(tok, mine, part, downdev, kind, z, has_down)
        copy_piece(tok, mine, AB, xdev, X, z, None)
        copy_piece(tok, mine, C, ydev, Y, z, None)
        copy_piece(tok, mine, C, xdev, X2, z, None)
        copy_piece(tok, mine, AB, ydev, Y2, z, None)

    def plane():
        await_piece(by, C, Y, z)
        send(by, C, xdev, DC, z)
        await_piece(bx, AB, X, z)
        send(bx, AB, ydev, DA, z)

    def ride_own():
        await_piece(by, AB, Y2, z)
        await_piece(bd, AB, DA, z)
        for part, kind in RIDES:
            copy_piece(held, plane_rows(z), part, updev, kind, z, has_up)
            copy_piece(held, plane_rows(z), part, downdev, kind, z, has_down)

    def sides(d):
        for up in (True, False):
            oz = z - d if up else z + d
            here = oz >= 0 if up else oz <= NZ - 1
            onward = jnp.logical_and(here, has_up if up else has_down)
            yield oz, here, (updev if up else downdev), (onward if d < NZ - 1 else False)

    def line(d):
        for oz, here, dev, onward in sides(d):
            b = block_of(oz, x, y)
            when(here)(functools.partial(await_piece, b, A, L, oz))
            if onward is not False:
                send(b, A, dev, L, oz, onward)
            send(b, A, xdev, X, oz, here)
            when(here)(functools.partial(await_piece, b, C, LC, oz))
            if onward is not False:
                send(b, C, dev, LC, oz, onward)
            send(b, C, ydev, Y, oz, here)
            send(b, C, xdev, X2, oz, here)
            send(b, A, ydev, Y2, oz, here)

    def cross(d):
        for oz, here, dev, onward in sides(d):
            ox, oy = block_of(oz, 1 - x, y), block_of(oz, x, 1 - y)
            when(here)(functools.partial(await_piece, ox, A, X, oz))
            send(ox, A, ydev, DA, oz, here)
            when(here)(functools.partial(await_piece, oy, C, Y, oz))
            send(oy, C, xdev, DC, oz, here)

    def ride(d):
        for oz, here, dev, onward in sides(d):
            for part, kind in RIDES:
                when(here)(functools.partial(await_rows, plane_rows(oz), part, kind, oz))
                if onward is not False:
                    copy_piece(held, plane_rows(oz), part, dev, kind, oz, onward)

    half = 2 * wrows
    mine_out = pl.ds(pl.multiple_of(me * half, half), half)

    def result_copy(oz, k):
        tx, ty = (x + k // 2) % 2, (y + k % 2) % 2
        return pltpu.make_async_remote_copy(
            src_ref=hid.at[rows_of(block_of(oz, tx, ty))], dst_ref=out.at[:, mine_out],
            send_sem=out_send.at[oz, k], recv_sem=out_recv.at[z, k],
            device_id=device(oz, tx, ty), device_id_type=MESH,
        )

    def multiply(oz):
        both = lax.dot_general(
            held[plane_rows(oz), :], w[...], (((1,), (1,)), ((), ())), preferred_element_type=jnp.float32
        )
        gate = both[:, :half]
        hid[plane_rows(oz), :] = (gate / (1.0 + jnp.exp(-gate)) * both[:, half:]).astype(jnp.bfloat16)

    def own_plane():
        await_piece(bx, C, X2, z)
        await_piece(bd, C, DC, z)
        multiply(z)
        for k in (3, 2, 1):
            result_copy(z, k).start()

    def other_planes(d, cond=None):
        for oz, here, _, _ in sides(d):
            def finish(oz=oz):
                diagonal = block_of(oz, 1 - x, 1 - y)
                await_piece(block_of(oz, 1 - x, y), C, X2, oz)
                await_piece(block_of(oz, x, 1 - y), A, Y2, oz)
                await_piece(diagonal, A, DA, oz)
                await_piece(diagonal, C, DC, oz)
                multiply(oz)
                for k in (3, 2, 1, 0):
                    result_copy(oz, k).start()
            when(here if cond is None else jnp.logical_and(here, cond))(finish)

    def weights():
        copies = []
        for i, (src, dst) in enumerate((
            (gw, w.at[own]), (uw, w.at[own_up]), (gm, masks.at[core]), (um, masks.at[2 + core]),
        )):
            copies.append(pltpu.make_async_remote_copy(
                src_ref=src, dst_ref=dst, send_sem=part_send.at[i], recv_sem=part_recv.at[i],
                device_id=partner, device_id_type=MESH,
            ))
        for copy in copies:
            copy.start()
        return copies

    def prune(copies):
        for copy in copies:
            copy.wait()
        for copy in locals_:
            copy.wait()
        step = 512
        block = width // masks.shape[2]
        row = lax.broadcasted_iota(jnp.int32, (8, masks.shape[2]), 0)
        table = jnp.zeros((8, masks.shape[2]), jnp.float32)
        for r in range(4):
            table = jnp.where(row == r, masks[r].astype(jnp.float32), table)
        table = table.astype(jnp.bfloat16)

        @pl.loop(0, width // step)
        def _(i):
            start = pl.multiple_of(i * step, step)
            where_ = lax.broadcasted_iota(jnp.int32, (masks.shape[2], step), 0)
            col = lax.broadcasted_iota(jnp.int32, (masks.shape[2], step), 1) + start
            first = where_ * block
            inside = jnp.logical_and(col >= first, col < first + block)
            select = jnp.where(inside, 1.0, 0.0).astype(jnp.bfloat16)
            wide[...] = jnp.dot(table, select, preferred_element_type=jnp.float32)
            for r in range(4):
                at = (pl.ds(r * wrows, wrows), pl.ds(start, step))
                keep = jnp.broadcast_to(wide[r:r + 1, :], (wrows, step))
                w[at] = (w[at].astype(jnp.float32) * keep).astype(jnp.bfloat16)

    begin()
    swaps = weights()
    plane()
    line(1)
    prune(swaps)
    line(2)
    ride_own()
    cross(1)
    line(3)
    own_plane()
    ride(1)
    cross(2)
    other_planes(1, at_end)
    ride(2)
    other_planes(1, jnp.logical_not(at_end))
    cross(3)
    other_planes(2)
    ride(3)
    other_planes(3)

    keep_own = pltpu.make_async_copy(hid.at[rows_of(me)], out.at[:, mine_out], out_local)
    keep_own.start()
    for copy, cond in sends:
        when(cond)(copy.wait_send)
    for oz in range(NZ):
        for k in range(4):
            def settle(oz=oz, k=k):
                sent = hid.at[rows_of(block_of(oz, (x + k // 2) % 2, (y + k % 2) % 2))]
                pltpu.make_async_copy(sent, sent, out_send.at[oz, k]).wait()
                source = block_of(oz, (x + k // 2) % 2, (y + k % 2) % 2)
                ref = out.at[:, pl.ds(pl.multiple_of(source * half, half), half)]
                pltpu.make_async_copy(ref, ref, out_recv.at[oz, k]).wait()
            when(z != oz if k == 0 else None)(settle)
    keep_own.wait()


NSENDS = 68


def shards(tokens, gate_weight, up_weight, gate_mask, up_mask):
    rows, width = tokens.shape
    wrows = gate_weight.shape[0]
    blocks = lax.axis_size("seq") * lax.axis_size("panel") // 2
    hidden = lax.axis_size("seq") * lax.axis_size("panel") * wrows
    dma = pltpu.SemaphoreType.DMA
    return pl.pallas_call(
        kernel,
        out_shape=jax.ShapeDtypeStruct((rows, hidden), jnp.bfloat16),
        in_specs=[pl.BlockSpec(memory_space=pl.ANY)] * 5,
        out_specs=pl.BlockSpec(memory_space=pl.ANY),
        scratch_shapes=[
            pltpu.VMEM((blocks * rows, width), jnp.bfloat16),
            pltpu.VMEM((4 * wrows, width), jnp.bfloat16),
            pltpu.VMEM((4, 1, gate_mask.shape[1]), jnp.int32),
            pltpu.VMEM((8, 512), jnp.float32),
            pltpu.VMEM((blocks * rows, 2 * wrows), jnp.bfloat16),
            dma((NKINDS, NZ)),
            dma((NSENDS,)),
            dma((4,)), dma((4,)), dma((5,)),
            dma((NZ, 4)), dma((NZ, 4)), dma,
        ],
        compiler_params=pltpu.CompilerParams(collective_id=0, has_side_effects=True),
    )(tokens, gate_weight, up_weight, gate_mask, up_mask)


def solution(mesh):
    spec = P(("seq", "panel"), None)
    fits = mesh.shape["seq"] == 2 * NZ and mesh.shape["panel"] == 4
    body = shards if fits else general_shards
    return jax.shard_map(
        body, mesh=mesh, in_specs=(spec,) * 5, out_specs=spec, check_vma=False
    )
```

time: 54 us -> 45.1 us (0.84)
  Pallas kernels: 52.3 us -> 43.4 us
    pallas_call x1, Pallas kernels: 52.3 us -> 43.4 us  [shards(): pl.pallas_call(kernel, out_shape=jax.ShapeDtypeStruct((rows, hidden), jnp...]
where the time goes in v2:
time: 45.1 us; the launch traced here: 44.9 us
  Pallas kernels  43.4 us (96%)
  local copies, waits for them, and re-layouts  1.47 us (3%)
    pallas_call x1, Pallas kernels, shards(): pl.pallas_call(kernel, out_shape=jax.ShapeDtypeStruct((rows, hidden), jnp...  43.4 us
    unnamed x1, local copies, waits for them, and re-layouts  1.47 us

profile of v2, /device:TPU:0, one launch (start us, length us, event | category | flops | bytes accessed | tf_op | source)
XLA Modules:
  0.0 44.9 jit_solution(14563269402022880490)
XLA Ops:
  0.0 43.4 %shard_map.55 = bf16[16,2048]{1,0:T(8,128)(2,1)} custom-call(bf16[16,8192]{1,0:T(8,128)(2,1)} %tok.1, bf16[64,8192]{1,0:T(8,128)(2,1)} %gw.1, bf16[64,8192]{1,0:T(8,128)(2,1)} %uw.1, s32[1,128]{1,0:T(1,128)} %gm.1, s32[1,128]{1,0:T(1,128)} %um.1), custom_call_target="tpu_custom_call" | custom-call | tf_op jit(solution)/shard_map/pallas_call | solution.py:339
  43.4 1.5 %copy.7 = bf16[16,2048]{1,0:T(8,128)(2,1)} copy(bf16[16,2048]{1,0:T(8,128)(2,1)} %shard_map.55) | data formatting | bytes 131072
